TPU v7x, 256 devices: a whole 4x4x8 slice. The times are simulated.
256 devices in a mesh: half: 2 (over core), row: 8 (over z_hi, x), col: 16 (over y, z_lo).
Axes of the slice: x: 4, y: 4, z: 8 (z_hi: 2, z_lo: 4; z = z_hi * 4 + z_lo), core: 2. Of those that a mesh axis runs over, the one named last changes fastest.
Arguments:
- parent_front: float32 [16384, 16384], P(('half', 'row'), 'col'), may hold values from -6 to 6
- child_blocks: float32 [2, 8192, 8192], P('half', 'row', 'col'), may hold values from -6 to 6
- row_maps: int32 [2, 8192], replicated, may hold values from 0 to 16383, as said below
- inverse_blocks: float32 [4, 128, 128], replicated, may hold values from -0.12 to 0.12
Outputs:
- updated_front: float32 [16384, 16384], P(('half', 'row'), 'col')
- panel_factor: bfloat16 [16384, 512], P(('half', 'row'))
Inputs may be any that keep to these rules, and one draw needn't show every extreme that they name: `row_maps`: each row lists 8192 distinct parent rows. In every aligned block of 512 entries of a row, at most 64 entries fall in one aligned block of 1024 parent rows, and that bound is reached in every such block; in every aligned block of 1024 entries, at most 128 fall in one aligned block of 1024 parent rows, and that bound is reached in every such block.
All inputs are finite; a program needn't handle non-finite values.
Results may differ from a plain program's by a relative error of at most 0.001.
Values sent between devices are 32-bit elements; how exact they have to be, the bound alone decides.
A program may use at most 128 MiB of HBM per device.

v0:
```python
import functools

import jax
import jax.numpy as jnp
from jax import lax
from jax.experimental import pallas as pl
from jax.experimental.pallas import tpu as pltpu
from jax.sharding import PartitionSpec as P

MESH = pl.DeviceIdType.MESH
F32 = jnp.float32
BF16 = jnp.bfloat16

SUB = 512
CAP = 64
LOC = 1024
GROUPS = 16
WIDTH = 128
BLOCKS = 4
PANEL = WIDTH * BLOCKS


def dot(left, right, dims):
    return lax.dot_general(left, right, (dims, ((), ())), preferred_element_type=F32)


def before(flags):
    size = flags.shape[-1]
    upper = jnp.arange(size)[:, None] < jnp.arange(size)[None, :]
    return jnp.dot(flags.astype(BF16), upper.astype(BF16), preferred_element_type=F32).astype(jnp.int32)


def send_slots(parents):
    targets = parents // LOC
    member = targets[:, None, :] == jnp.arange(GROUPS, dtype=jnp.int32)[None, :, None]
    rank = jnp.sum(before(member) * member.astype(jnp.int32), axis=1)
    return targets, rank


def landing(parents, mine):
    member = parents // LOC == mine
    rank = jnp.where(member, before(member), -1)
    hit = rank[:, :, None, :] == jnp.arange(CAP, dtype=jnp.int32)[None, None, :, None]
    return jnp.sum(jnp.where(hit, (parents % LOC + 1)[:, :, None, :], 0), axis=-1) - 1


def place():
    half, row, col = lax.axis_index("half"), lax.axis_index("row"), lax.axis_index("col")
    return half, row // 4, row % 4, col // 4, col % 4


def device(half, z_hi, x, y, z_lo):
    return {"half": half, "row": z_hi * 4 + x, "col": y * 4 + z_lo}


def group_tree(half, z_hi, x, y, z_lo, src_half, src_z, src_x):
    away = (x - src_x + 4) % 4
    lead = half == src_half
    source = lead & (z_hi == src_z) & (away == 0)
    children = [
        (source, device(half, 1 - z_hi, x, y, z_lo)),
        (lead & (away <= 1), device(half, z_hi, (x + 1) % 4, y, z_lo)),
        (lead & (away == 0), device(half, z_hi, (x + 3) % 4, y, z_lo)),
        (lead, device(1 - half, z_hi, x, y, z_lo)),
    ]
    up_x = jnp.where(away == 3, (x + 1) % 4, (x + 3) % 4)
    parent_half = jnp.where(lead, half, 1 - half)
    parent_z = jnp.where(lead & (away == 0), 1 - z_hi, z_hi)
    parent_x = jnp.where(lead & (away != 0), up_x, x)
    parent = device(parent_half, parent_z, parent_x, y, z_lo)
    hops = jnp.where(away == 3, 1, away) + jnp.where(lead, 0, 1) + jnp.where(z_hi == src_z, 0, 2)
    return source, children, parent, hops


def z_first_tree(half, z_hi, x, y, z_lo):
    at = lambda y2, z2: device(half, z_hi, x, y2, z2)
    children = [
        ((y == 0) & (z_lo < 3), at(0, z_lo + 1)),
        ((y <= 1) & (z_lo >= 1), at(y + 1, z_lo)),
        ((y == 0) & (z_lo >= 1), at(3, z_lo)),
        ((y >= 1) & (z_lo == 1), at(y, 0)),
    ]
    back = (z_lo == 0) & (y >= 1)
    parent_y = jnp.where(back, y, jnp.where(y == 2, 1, 0))
    parent_z = jnp.where(back, 1, jnp.where(y == 0, z_lo - 1, z_lo))
    turn = jnp.where(y == 3, 1, y)
    hops = jnp.where(back, turn + 2, turn + z_lo)
    return children, at(parent_y, parent_z), hops


def y_first_tree(half, z_hi, x, y, z_lo):
    at = lambda y2, z2: device(half, z_hi, x, y2, z2)
    children = [
        ((z_lo == 0) & (y <= 1), at(y + 1, 0)),
        ((z_lo == 0) & (y == 0), at(3, 0)),
        ((y >= 1) & (z_lo < 3), at(y, z_lo + 1)),
        ((y == 1) & (z_lo >= 1), at(0, z_lo)),
    ]
    back = (y == 0) & (z_lo >= 1)
    parent_y = jnp.where(z_lo == 0, jnp.where(y == 2, 1, 0), jnp.where(y == 0, 1, y))
    parent_z = jnp.where((z_lo == 0) | back, z_lo, z_lo - 1)
    turn = jnp.where(y == 3, 1, y)
    hops = jnp.where(back, z_lo + 2, turn + z_lo)
    return children, at(parent_y, parent_z), hops


def count(children):
    total = 0
    for cond, _ in children:
        total = total + cond.astype(jnp.int32)
    return total


def wait_for(barrier, signals):
    @pl.when(signals > 0)
    def _():
        pl.semaphore_wait(barrier, signals)


def remote(src, dst, send, recv, target):
    return pltpu.make_async_remote_copy(
        src_ref=src, dst_ref=dst, send_sem=send, recv_sem=recv, device_id=target, device_id_type=MESH
    )


def split(value):
    high = value.astype(BF16)
    return high, (value - high.astype(F32)).astype(BF16)


def outer(left, right):
    left_high, left_low = split(left)
    right_high, right_low = split(right)
    dims = ((1,), (1,))
    return dot(left_high, right_high, dims) + (dot(left_high, right_low, dims) + dot(left_low, right_high, dims))


def panel_kernel(a_ref, inv_ref, f_ref, d_ref, l_ref, send, recv, own):
    half, z_hi, x, y, z_lo = place()
    source, children, parent, _ = group_tree(half, z_hi, x, y, z_lo, 0, 0, 0)
    active = (y == 0) & (z_lo == 0)
    barrier = pltpu.get_barrier_semaphore()

    @pl.when(active)
    def _():
        @pl.when(jnp.logical_not(source))
        def _():
            pl.semaphore_signal(barrier, inc=1, device_id=parent, device_id_type=MESH)

        wait_for(barrier, count(children))

        def piece(ref, block):
            return ref.at[pl.ds(block * WIDTH, WIDTH), pl.ds(0, block * WIDTH)]

        def copy(block, number):
            return remote(
                piece(d_ref, block), piece(d_ref, block), send.at[number, block - 1], recv.at[block - 1], children[number][1]
            )

        for block in range(1, BLOCKS):
            @pl.when(source)
            def _():
                mine = pltpu.make_async_copy(piece(a_ref, block), piece(d_ref, block), own)
                mine.start()
                mine.wait()

            @pl.when(jnp.logical_not(source))
            def _():
                copy(block, 0).wait_recv()

            for number, (cond, _) in enumerate(children):
                @pl.when(cond)
                def _():
                    copy(block, number).start()

        lower = lax.broadcasted_iota(jnp.int32, (WIDTH, WIDTH), 0) >= lax.broadcasted_iota(jnp.int32, (WIDTH, WIDTH), 1)
        for block in range(BLOCKS):
            inverse = jnp.where(lower, inv_ref[block], 0.0)
            here = pl.ds(block * WIDTH, WIDTH)
            done = pl.ds(0, block * WIDTH)
            current = a_ref[:, here]
            if block > 0:
                above = l_ref[here, done]
                current = current - outer(f_ref[:, done], above)
            f_ref[:, here] = outer(current, inverse)
            if block + 1 < BLOCKS:
                below = pl.ds((block + 1) * WIDTH, PANEL - (block + 1) * WIDTH)
                current = d_ref[below, here]
                if block > 0:
                    current = current - outer(l_ref[below, done], above)
                l_ref[below, here] = outer(current, inverse)

        for block in range(1, BLOCKS):
            for number, (cond, _) in enumerate(children):
                @pl.when(cond)
                def _():
                    copy(block, number).wait_send()


def panel(a, inverse_blocks):
    return pl.pallas_call(
        panel_kernel,
        out_shape=jax.ShapeDtypeStruct(a.shape, F32),
        in_specs=[pl.BlockSpec(memory_space=pltpu.VMEM)] * 2,
        out_specs=pl.BlockSpec(memory_space=pltpu.VMEM),
        scratch_shapes=[
            pltpu.VMEM((PANEL, PANEL), F32),
            pltpu.VMEM((PANEL, PANEL), F32),
            pltpu.SemaphoreType.DMA((4, BLOCKS - 1)),
            pltpu.SemaphoreType.DMA((BLOCKS - 1,)),
            pltpu.SemaphoreType.DMA,
        ],
        compiler_params=pltpu.CompilerParams(collective_id=0, has_side_effects=True, vmem_limit_bytes=24 * 2**20),
        name="panel",
    )(a, inverse_blocks)


CHUNK = 32
STEP = 2


def spread_kernel(f_ref, row_ref, col_ref, recv_z, recv_y, recv_g, send_z, send_y, send_g, own):
    half, z_hi, x, y, z_lo = place()
    side = row_ref.shape[0] // 2
    chunks = side // CHUNK
    tree_z, parent_z, hops_z = z_first_tree(half, z_hi, x, y, z_lo)
    tree_y, parent_y, hops_y = y_first_tree(half, z_hi, x, y, z_lo)
    source, tree_g, parent_g, hops_g = group_tree(half, z_hi, x, y, z_lo, y // 2, y % 2, z_lo)
    root = (y == 0) & (z_lo == 0)
    barrier = pltpu.get_barrier_semaphore()

    @pl.when(jnp.logical_not(root))
    def _():
        pl.semaphore_signal(barrier, inc=1, device_id=parent_z, device_id_type=MESH)
        pl.semaphore_signal(barrier, inc=1, device_id=parent_y, device_id_type=MESH)

    @pl.when(jnp.logical_not(source))
    def _():
        pl.semaphore_signal(barrier, inc=1, device_id=parent_g, device_id_type=MESH)

    @pl.when(root)
    def _():
        mine = pltpu.make_async_copy(f_ref, row_ref, own)
        mine.start()
        mine.wait()

    wait_for(barrier, count(tree_z) + count(tree_y) + count(tree_g))

    def rows(number):
        return pl.ds(pl.multiple_of(number * CHUNK, CHUNK), CHUNK)

    def forward(src, dst, number, tree, sends, recv):
        for slot, (cond, target) in enumerate(tree):
            @pl.when(cond)
            def _():
                remote(src.at[rows(number)], dst.at[rows(number)], sends.at[slot], recv, target).start()

    def along_row(number, offset, tree, sends, recv):
        @pl.when((number >= 0) & (number < chunks))
        def _():
            @pl.when(jnp.logical_not(root))
            def _():
                at = row_ref.at[rows(offset + number)]
                remote(at, at, sends.at[0], recv.at[number], tree[0][1]).wait_recv()

            forward(row_ref, row_ref, offset + number, tree, sends, recv.at[number])

            @pl.when(source)
            def _():
                forward(row_ref, col_ref, offset + number, tree_g, send_g, recv_g.at[offset + number])

    def along_col(number, offset):
        @pl.when((number >= 0) & (number < chunks) & jnp.logical_not(source))
        def _():
            at = col_ref.at[rows(offset + number)]
            remote(at, at, send_g.at[0], recv_g.at[offset + number], tree_g[0][1]).wait_recv()
            forward(col_ref, col_ref, offset + number, tree_g, send_g, recv_g.at[offset + number])

    start_z, start_y, start_g = hops_z * STEP, hops_y * STEP, hops_g * STEP

    def body(step, carry):
        along_row(step - start_z, 0, tree_z, send_z, recv_z)
        along_row(step - start_y, chunks, tree_y, send_y, recv_y)
        along_col(step - start_z - start_g, 0)
        along_col(step - start_y - start_g, chunks)
        return carry

    lax.fori_loop(0, chunks + STEP * 11, body, 0)

    @pl.when(source)
    def _():
        mine = pltpu.make_async_copy(row_ref, col_ref, own)
        mine.start()
        mine.wait()

    def drain(tree, sends, size):
        at = row_ref.at[pl.ds(0, size)]
        for slot, (cond, target) in enumerate(tree):
            @pl.when(cond)
            def _():
                remote(at, at, sends.at[slot], recv_z.at[0], target).wait_send()

    drain(tree_z, send_z, side)
    drain(tree_y, send_y, side)
    drain(tree_g, send_g, 2 * side)


def spread(f):
    chunks = f.shape[0] // 2 // CHUNK
    return pl.pallas_call(
        spread_kernel,
        out_shape=[jax.ShapeDtypeStruct(f.shape, F32)] * 2,
        in_specs=[pl.BlockSpec(memory_space=pltpu.VMEM)],
        out_specs=[pl.BlockSpec(memory_space=pltpu.VMEM)] * 2,
        scratch_shapes=[
            pltpu.SemaphoreType.DMA((chunks,)),
            pltpu.SemaphoreType.DMA((chunks,)),
            pltpu.SemaphoreType.DMA((2 * chunks,)),
            pltpu.SemaphoreType.DMA((4,)),
            pltpu.SemaphoreType.DMA((4,)),
            pltpu.SemaphoreType.DMA((4,)),
            pltpu.SemaphoreType.DMA,
        ],
        compiler_params=pltpu.CompilerParams(collective_id=1, has_side_effects=True, vmem_limit_bytes=24 * 2**20),
        name="spread",
    )(f)


def exchange_kernel(
    x_ref, parent_ref, row_ref, col_ref, row_land_ref, col_land_ref, out_ref,
    held, packed, landed, pick, by_col, parts, by_row, put,
    own, first, ring_sent, ring_got, sent, got, kept,
):
    half, z_hi, x, y, z_lo = place()
    z = z_hi * 4 + z_lo
    mid = held.shape[1] // 2
    tile = 256
    rows_dims = ((1,), (1,))
    up, down = (z + 1) % 8, (z + 7) % 8
    above = device(half, up // 4, x, y, up % 4)
    below = device(half, down // 4, x, y, down % 4)

    def peer(number):
        return device((half + number // 16) % 2, z_hi, (x + number // 4) % 4, (y + number) % 4, z_lo)

    mine = pltpu.make_async_copy(x_ref, held.at[0], own)
    mine.start()
    front = pltpu.make_async_copy(parent_ref, out_ref, first)
    front.start()
    barrier = pltpu.get_barrier_semaphore()
    for target in (above, below):
        pl.semaphore_signal(barrier, inc=1, device_id=target, device_id_type=MESH)

    def greet(number, carry):
        pl.semaphore_signal(barrier, inc=1, device_id=peer(number), device_id_type=MESH)
        return carry

    lax.fori_loop(1, 32, greet, 0)
    mine.wait()
    pl.semaphore_wait(barrier, 33)

    def at_of(number):
        return jnp.where(number % 2 == 1, 8 - (number + 1) // 2, number // 2)

    def part(at, side):
        return held.at[at, pl.ds(side * mid, mid), :]

    def ring(at, side, way):
        to = (at + 7) % 8 if way == 0 else (at + 1) % 8
        return remote(
            part(at, side), part(to, side), ring_sent.at[way, at, side], ring_got.at[to, side], (above, below)[way]
        )

    def arrived(at, side):
        remote(part(at, side), part(at, side), ring_sent.at[0, at, side], ring_got.at[at, side], above).wait_recv()

    def message(number, to):
        to_half, to_x, to_y = (half + to // 16) % 2, (x + to // 4) % 4, (y + to) % 4
        src = packed.at[
            number % 4,
            pl.ds(pl.multiple_of(to_y * CAP, CAP), CAP),
            pl.ds(pl.multiple_of((to_half * 4 + to_x) * 128, 128), 128),
        ]
        dst = landed.at[
            at_of(number), half, pl.ds(pl.multiple_of(y * CAP, CAP), CAP), pl.ds(pl.multiple_of(x * 128, 128), 128)
        ]
        return src, dst

    def deliver(number):
        src, dst = message(number, 0)
        pltpu.make_async_copy(src, dst, kept.at[number]).start()

        def one(to, carry):
            src, dst = message(number, to)
            remote(src, dst, sent.at[number], got.at[number], peer(to)).start()
            return carry

        lax.fori_loop(1, 32, one, 0)

    def others():
        return out_ref.at[pl.ds(0, 31 * 8), :]

    def gone(number):
        remote(others(), others(), sent.at[number], got.at[number], above).wait_send()

    def landed_all(number):
        remote(others(), others(), sent.at[number], got.at[number], above).wait_recv()
        src, dst = message(number, 0)
        pltpu.make_async_copy(src, dst, kept.at[number]).wait()

    def pack(number):
        at = at_of(number)
        there = (z + at) % 8
        slots = lax.broadcasted_iota(jnp.int32, (4 * CAP, SUB), 0)
        col_pick = (slots == col_ref[there % 4]).astype(F32).astype(BF16)

        def columns(step, carry):
            here = pl.ds(pl.multiple_of(step * tile, tile), tile)
            high, low = split(held[at, here, :])
            by_col[: 4 * CAP, here] = dot(col_pick, high, rows_dims).astype(BF16)
            by_col[4 * CAP :, here] = dot(col_pick, low, rows_dims).astype(BF16)
            return carry

        lax.fori_loop(0, LOC // tile, columns, 0)

        def rows(step, carry):
            here = pl.ds(pl.multiple_of(step * tile, tile), tile)
            both = dot(by_col[...], pick[there // 4, here, :], rows_dims)
            packed[number % 4, :, here] = both[: 4 * CAP] + both[4 * CAP :]
            return carry

        lax.fori_loop(0, LOC // tile, rows, 0)

    def rows_of(number, child, step):
        source = (z + at_of(number)) % 8 // 4
        places = lax.broadcasted_iota(jnp.int32, (tile, SUB), 0) + step * tile
        row_put = (places == row_land_ref[child, source]).astype(F32).astype(BF16)
        return dot(row_put, parts[child], rows_dims).astype(BF16)

    def take(number):
        landed_all(number)
        for child in range(2):
            high, low = split(landed[at_of(number), child])
            parts[child, : 4 * CAP] = high
            parts[child, 4 * CAP :] = low

    def unpack_first(number):
        take(number)

        def rows(step, carry):
            here = pl.ds(pl.multiple_of(step * tile, tile), tile)
            for child in range(2):
                by_row[at_of(number) % 4, child, here, :] = rows_of(number, child, step)
            return carry

        lax.fori_loop(0, LOC // tile, rows, 0)

    def unpack_second(number, carry):
        source = (z + at_of(number)) % 4
        for child in range(2):
            places = lax.broadcasted_iota(jnp.int32, (LOC, 4 * CAP), 0)
            col_put = (places == col_land_ref[child, source]).astype(F32).astype(BF16)
            put[child, :, : 4 * CAP] = col_put
            put[child, :, 4 * CAP :] = col_put
        take(number)

        def rows(step, carry):
            here = pl.ds(pl.multiple_of(step * tile, tile), tile)
            total = out_ref[here, :]
            for child in range(2):
                both = by_row[at_of(number) % 4, child, here, :] + rows_of(number, child, step)
                total = total + dot(both, put[child], rows_dims)
            out_ref[here, :] = total
            return carry

        lax.fori_loop(0, LOC // tile, rows, 0)
        return carry

    for side in range(2):
        for way in range(2):
            ring(0, side, way).start()
    for source in range(2):
        slots = lax.broadcasted_iota(jnp.int32, pick.shape[1:], 0)
        pick[source] = (slots == row_ref[source]).astype(F32).astype(BF16)
    front.wait()

    def event(number, carry):
        @pl.when(number % 2 == 1)
        def _():
            step = (number + 1) // 2
            for side in range(2):
                arrived(8 - step, side)

                @pl.when(step < 4 - side)
                def _():
                    ring(8 - step, side, 0).start()

                @pl.when(step < 4)
                def _():
                    arrived(step, side)

                    @pl.when(step < 3 + side)
                    def _():
                        ring(step, side, 1).start()

        @pl.when(number >= 4)
        def _():
            gone(number - 4)

        pack(number)

        @pl.when((number >= 3) & (number < 7))
        def _():
            unpack_first(number - 3)

        deliver(number)
        return carry

    lax.fori_loop(0, 8, event, 0)
    lax.fori_loop(4, 8, unpack_second, 0)

    def settle(number, carry):
        gone(number)
        return carry

    lax.fori_loop(4, 8, settle, 0)
    for side in range(2):
        for at in (0, 7, 6, 5)[: 4 - side]:
            ring(at, side, 0).wait_send()
        for at in (0, 1, 2, 3)[: 3 + side]:
            ring(at, side, 1).wait_send()


def exchange(block, parent, row_slots, col_slots, row_land, col_land):
    rows, cols = block.shape
    return pl.pallas_call(
        exchange_kernel,
        out_shape=jax.ShapeDtypeStruct(parent.shape, F32),
        in_specs=[pl.BlockSpec(memory_space=pl.ANY)] * 2 + [pl.BlockSpec(memory_space=pltpu.VMEM)] * 4,
        out_specs=pl.BlockSpec(memory_space=pltpu.VMEM),
        scratch_shapes=[
            pltpu.VMEM((8, rows, cols), F32),
            pltpu.VMEM((4, 4 * CAP, LOC), F32),
            pltpu.VMEM((8, 2, 4 * CAP, SUB), F32),
            pltpu.VMEM((2, LOC, rows), BF16),
            pltpu.VMEM((8 * CAP, LOC), BF16),
            pltpu.VMEM((2, 8 * CAP, SUB), BF16),
            pltpu.VMEM((4, 2, LOC, 8 * CAP), BF16),
            pltpu.VMEM((2, LOC, 8 * CAP), BF16),
            pltpu.SemaphoreType.DMA,
            pltpu.SemaphoreType.DMA,
            pltpu.SemaphoreType.DMA((2, 8, 2)),
            pltpu.SemaphoreType.DMA((8, 2)),
            pltpu.SemaphoreType.DMA((8,)),
            pltpu.SemaphoreType.DMA((8,)),
            pltpu.SemaphoreType.DMA((8,)),
        ],
        compiler_params=pltpu.CompilerParams(collective_id=2, has_side_effects=True, vmem_limit_bytes=63 * 2**20),
        name="exchange",
    )(block, parent, row_slots, col_slots, row_land, col_land)


def local(parent_front, child_blocks, row_maps, inverse_blocks):
    half, row, col = lax.axis_index("half"), lax.axis_index("row"), lax.axis_index("col")
    group = half * 8 + row
    maps = row_maps.reshape(2, -1, SUB)

    mine = lax.dynamic_index_in_dim(maps, half, 0, keepdims=False)
    shards = mine.reshape(2, 4, 2 * SUB)
    target, rank = send_slots(lax.dynamic_index_in_dim(shards, row % 4, 1, keepdims=False).reshape(4, SUB))
    target, rank = target.reshape(2, 2, SUB), rank.reshape(2, 2, SUB)
    side = jnp.arange(2, dtype=jnp.int32)[:, None]
    slot = (((target // 8) * 4 + target % 4) * 2 + side) * CAP + rank
    row_slots = jnp.where(target // 4 % 2 == row // 4, slot, -1).reshape(2, 1, 2 * SUB)
    target, rank = send_slots(lax.dynamic_index_in_dim(mine.reshape(4, 4, SUB), col // 4, 0, keepdims=False))
    col_slots = jnp.where(target % 4 == col % 4, (target // 4) * CAP + rank, -1).reshape(4, 1, SUB)

    row_land = landing(maps, group).reshape(2, 2, 1, SUB)
    col_land = landing(maps, col).reshape(2, 4, 4, CAP).transpose(0, 2, 1, 3).reshape(2, 4, 1, 4 * CAP)
    assembled = exchange(child_blocks[0], parent_front, row_slots, col_slots, row_land, col_land)

    factor = panel(assembled[:, :PANEL], inverse_blocks)
    factor_rows, factor_cols = spread(factor)
    product = lax.dot_general(
        factor_rows, factor_cols, (((1,), (1,)), ((), ())), precision=lax.Precision.HIGH, preferred_element_type=F32
    )
    return assembled - product, factor_rows.astype(BF16)


def solution(mesh):
    in_specs = (P(("half", "row"), "col"), P("half", "row", "col"), P(), P())
    out_specs = (P(("half", "row"), "col"), P(("half", "row"), None))
    return jax.shard_map(local, mesh=mesh, in_specs=in_specs, out_specs=out_specs, check_vma=False)
```

profile of v0, /device:TPU:73, one launch (start us, length us, event | category | flops | bytes accessed | tf_op | source)
XLA Modules:
  0.0 311.0 jit_solution(6784364033548999478)
XLA Ops:
  0.7 1.1 fusion.5
  1.8 1.1 fusion.4
  3.0 0.9 fusion.11
  3.9 1.2 select_reduce_fusion
  5.1 0.7 reshape.264.col_land_ref
  5.7 0.7 sub.67.row_land_ref
  6.4 0.9 copy.25
  7.4 0.2 fusion.3
  7.6 0.7 compare_select_fusion.2.col_ref
  8.4 0.2 fusion.2
  8.6 0.8 compare_select_fusion.3.row_ref
  9.4 197.3 %exchange.1 = f32[1024,1024]{1,0:T(8,128)} custom-call(f32[1024,512]{1,0:T(8,128)} %bitcast.49, f32[1024,1024]{1,0:T(8,128)} %parent_ref.1, s32[2,1,1024]{2,1,0:T(1,128)} %compare_select_fusion.3.row_ref, s32[4,1,512]{2,1,0:T(1,128)} %compare_select_fusion.2.col_ref, s32[2,2,1,512]{3,2,1,0:T(1,128)} %sub.67.row_land_ref, s32[2,4,1,256]{3,2,1,0:T(1,128)} %reshape.264.col_land_ref), custom_call_target="tpu_custom_call" | custom-call | tf_op jit(solution)/shard_map/exchange/pallas_call | solution.py:536
  206.7 0.0 copy-start
  206.8 1.8 slice.3.a_ref
  208.6 0.0 copy-done
  208.6 0.0 copy-start.1
  208.6 0.3 panel.1.f_ref
  208.9 95.9 %spread.1 = (f32[1024,512]{1,0:T(8,128)S(1)}, f32[1024,512]{1,0:T(8,128)S(1)}) custom-call(f32[1024,512]{1,0:T(8,128)S(1)} %panel.1.f_ref), custom_call_target="tpu_custom_call" | custom-call | tf_op jit(solution)/shard_map/spread/pallas_call | solution.py:310
  304.8 0.0 copy-done.1
  304.8 5.0 %convolution_subtract_fusion = f32[1024,1024]{1,0:T(8,128)} fusion(f32[1024,1024]{1,0:T(8,128)S(1)} %copy-done.1, f32[1024,512]{1,0:T(8,128)S(1)} %get-tuple-element.4, f32[1024,512]{1,0:T(8,128)S(1)} %get-tuple-element.5), kind=kOutput, calls=%fused_computation.4 | convolution fusion | flops 3222274048 | bytes 12582912 | tf_op jit(solution)/shard_map/dot_general | solution.py:584
  309.9 1.1 convert_element_type.14
  (12 shorter events, 0.2 us)
Async XLA Ops:
  206.7 1.8 copy-start
  208.6 96.2 %copy-start.1 = (f32[1024,1024]{1,0:T(8,128)S(1)}, f32[1024,1024]{1,0:T(8,128)}, u32[]{:S(2)}) copy-start(f32[1024,1024]{1,0:T(8,128)} %exchange.1) | copy-start | bytes 12582916
where the time goes:
time: 311 us
  Pallas kernels  294 us (95%)
  matrix products  7.77 us (2%)
  other arithmetic  4.68 us (2%)
  local copies, waits for them, and re-layouts  4.16 us (1%)
    pallas_call x1, Pallas kernels, exchange(): pl.pallas_call(exchange_kernel, out_shape=jax.ShapeDtypeStruct(parent.sha...  197 us
    pallas_call x1, Pallas kernels, spread(): pl.pallas_call(spread_kernel, out_shape=[jax.ShapeDtypeStruct(f.shape, F3...  95.9 us

commit v1 on v0

--- a/solution.py
+++ b/solution.py
@@ -225,8 +225,15 @@
     chunks = side // CHUNK
     tree_z, parent_z, hops_z = z_first_tree(half, z_hi, x, y, z_lo)
     tree_y, parent_y, hops_y = y_first_tree(half, z_hi, x, y, z_lo)
-    source, tree_g, parent_g, hops_g = group_tree(half, z_hi, x, y, z_lo, y // 2, y % 2, z_lo)
     root = (y == 0) & (z_lo == 0)
+    lead, near = half == y // 2, z_hi == y % 2
+    source = lead & near & (x == z_lo)
+    column = [
+        device(half, 1 - z_hi, x, y, z_lo),
+        device(half, z_hi, (x + 1) % 4, y, z_lo),
+        device(half, z_hi, (x + 3) % 4, y, z_lo),
+        device(1 - half, z_hi, x, y, z_lo),
+    ]
     barrier = pltpu.get_barrier_semaphore()
 
     @pl.when(jnp.logical_not(root))
@@ -234,9 +241,8 @@
         pl.semaphore_signal(barrier, inc=1, device_id=parent_z, device_id_type=MESH)
         pl.semaphore_signal(barrier, inc=1, device_id=parent_y, device_id_type=MESH)
 
-    @pl.when(jnp.logical_not(source))
-    def _():
-        pl.semaphore_signal(barrier, inc=1, device_id=parent_g, device_id_type=MESH)
+    for target in column:
+        pl.semaphore_signal(barrier, inc=1, device_id=target, device_id_type=MESH)
 
     @pl.when(root)
     def _():
@@ -244,7 +250,7 @@
         mine.start()
         mine.wait()
 
-    wait_for(barrier, count(tree_z) + count(tree_y) + count(tree_g))
+    pl.semaphore_wait(barrier, count(tree_z) + count(tree_y) + len(column))
 
     def rows(number):
         return pl.ds(pl.multiple_of(number * CHUNK, CHUNK), CHUNK)
@@ -253,7 +259,22 @@
         for slot, (cond, target) in enumerate(tree):
             @pl.when(cond)
             def _():
-                remote(src.at[rows(number)], dst.at[rows(number)], sends.at[slot], recv, target).start()
+                remote(src.at[rows(number)], dst.at[rows(number)], sends(slot), recv, target).start()
+
+    def turn(away):
+        return jnp.where(away == 3, 1, away)
+
+    def column_tree(bridge):
+        from_source = (x - z_lo + 4) % 4
+        away = jnp.where(near, from_source, (from_source - bridge + 4) % 4)
+        children = [
+            (lead & near & (from_source == bridge), column[0]),
+            (lead & (away <= 1), column[1]),
+            (lead & (away == 0), column[2]),
+            (lead, column[3]),
+        ]
+        hops = turn(away) + jnp.where(lead, 0, 1) + jnp.where(near, 0, 2 + turn(bridge))
+        return children, hops
 
     def along_row(number, offset, tree, sends, recv):
         @pl.when((number >= 0) & (number < chunks))
@@ -263,29 +284,39 @@
                 at = row_ref.at[rows(offset + number)]
                 remote(at, at, sends.at[0], recv.at[number], tree[0][1]).wait_recv()
 
-            forward(row_ref, row_ref, offset + number, tree, sends, recv.at[number])
+            forward(row_ref, row_ref, offset + number, tree, lambda slot: sends.at[slot], recv.at[number])
 
             @pl.when(source)
             def _():
-                forward(row_ref, col_ref, offset + number, tree_g, send_g, recv_g.at[offset + number])
-
-    def along_col(number, offset):
-        @pl.when((number >= 0) & (number < chunks) & jnp.logical_not(source))
-        def _():
-            at = col_ref.at[rows(offset + number)]
-            remote(at, at, send_g.at[0], recv_g.at[offset + number], tree_g[0][1]).wait_recv()
-            forward(col_ref, col_ref, offset + number, tree_g, send_g, recv_g.at[offset + number])
-
-    start_z, start_y, start_g = hops_z * STEP, hops_y * STEP, hops_g * STEP
+                along = offset + number
+                forward(row_ref, col_ref, along, column_tree(number % 4)[0], lambda slot: send_g.at[slot, along], recv_g.at[along])
+
+    def along_col(step, offset):
+        def one(bridge, carry):
+            children, hops = column_tree(bridge)
+            number = step - hops * STEP
+
+            @pl.when((number >= 0) & (number < chunks) & (number % 4 == bridge) & jnp.logical_not(source))
+            def _():
+                along = offset + number
+                at = col_ref.at[rows(along)]
+                remote(at, at, send_g.at[0, along], recv_g.at[along], column[0]).wait_recv()
+                forward(col_ref, col_ref, along, children, lambda slot: send_g.at[slot, along], recv_g.at[along])
+
+            return carry
+
+        lax.fori_loop(0, 4, one, 0)
+
+    start_z, start_y = hops_z * STEP, hops_y * STEP
 
     def body(step, carry):
         along_row(step - start_z, 0, tree_z, send_z, recv_z)
         along_row(step - start_y, chunks, tree_y, send_y, recv_y)
-        along_col(step - start_z - start_g, 0)
-        along_col(step - start_y - start_g, chunks)
+        along_col(step - start_z, 0)
+        along_col(step - start_y, chunks)
         return carry
 
-    lax.fori_loop(0, chunks + STEP * 11, body, 0)
+    lax.fori_loop(0, chunks + STEP * 13, body, 0)
 
     @pl.when(source)
     def _():
@@ -293,16 +324,26 @@
         mine.start()
         mine.wait()
 
-    def drain(tree, sends, size):
-        at = row_ref.at[pl.ds(0, size)]
+    def drain(tree, sends):
+        at = row_ref.at[pl.ds(0, side)]
         for slot, (cond, target) in enumerate(tree):
             @pl.when(cond)
             def _():
                 remote(at, at, sends.at[slot], recv_z.at[0], target).wait_send()
 
-    drain(tree_z, send_z, side)
-    drain(tree_y, send_y, side)
-    drain(tree_g, send_g, 2 * side)
+    drain(tree_z, send_z)
+    drain(tree_y, send_y)
+
+    def drain_column(number, carry):
+        at = row_ref.at[rows(number)]
+        for slot, (cond, target) in enumerate(column_tree(number % 4)[0]):
+            @pl.when(cond)
+            def _():
+                remote(at, at, send_g.at[slot, number], recv_z.at[0], target).wait_send()
+
+        return carry
+
+    lax.fori_loop(0, 2 * chunks, drain_column, 0)
 
 
 def spread(f):
@@ -318,7 +359,7 @@
             pltpu.SemaphoreType.DMA((2 * chunks,)),
             pltpu.SemaphoreType.DMA((4,)),
             pltpu.SemaphoreType.DMA((4,)),
-            pltpu.SemaphoreType.DMA((4,)),
+            pltpu.SemaphoreType.DMA((4, 2 * chunks)),
             pltpu.SemaphoreType.DMA,
         ],
         compiler_params=pltpu.CompilerParams(collective_id=1, has_side_effects=True, vmem_limit_bytes=24 * 2**20),
@@ -328,8 +369,8 @@
 
 def exchange_kernel(
     x_ref, parent_ref, row_ref, col_ref, row_land_ref, col_land_ref, out_ref,
-    held, packed, landed, pick, by_col, parts, by_row, put,
-    own, first, ring_sent, ring_got, sent, got, kept,
+    held, strained, passed, packed, landed, pick, by_col, parts, by_row, put,
+    own, first, ring_sent, ring_got, less_sent, less_got, sent, got, kept,
 ):
     half, z_hi, x, y, z_lo = place()
     z = z_hi * 4 + z_lo
@@ -362,10 +403,14 @@
     def at_of(number):
         return jnp.where(number % 2 == 1, 8 - (number + 1) // 2, number // 2)
 
+    def spot(at):
+        return at - at // 7 * 3
+
     def part(at, side):
-        return held.at[at, pl.ds(side * mid, mid), :]
-
-    def ring(at, side, way):
+        return held.at[spot(at), pl.ds(side * mid, mid), :]
+
+
+    def ring(at, way, side):
         to = (at + 7) % 8 if way == 0 else (at + 1) % 8
         return remote(
             part(at, side), part(to, side), ring_sent.at[way, at, side], ring_got.at[to, side], (above, below)[way]
@@ -373,6 +418,22 @@
 
     def arrived(at, side):
         remote(part(at, side), part(at, side), ring_sent.at[0, at, side], ring_got.at[at, side], above).wait_recv()
+
+    def less(place, way):
+        return remote(
+            passed.at[place], strained.at[place], less_sent.at[place], less_got.at[place], (above, below)[way]
+        )
+
+    def columns_of(which, at, here):
+        slots = lax.broadcasted_iota(jnp.int32, (4 * CAP, SUB), 0)
+        col_pick = (slots == col_ref[which, (z + at) % 4]).astype(F32).astype(BF16)
+        high, low = split(held[spot(at), here, :])
+        return dot(col_pick, high, rows_dims), dot(col_pick, low, rows_dims)
+
+    def strain(at, side, way, place):
+        high, low = columns_of(1 + way, at, pl.ds(side * mid, mid))
+        passed[place] = high + low
+        less(place, way).start()
 
     def message(number, to):
         to_half, to_x, to_y = (half + to // 16) % 2, (x + to // 4) % 4, (y + to) % 4
@@ -411,17 +472,21 @@
     def pack(number):
         at = at_of(number)
         there = (z + at) % 8
-        slots = lax.broadcasted_iota(jnp.int32, (4 * CAP, SUB), 0)
-        col_pick = (slots == col_ref[there % 4]).astype(F32).astype(BF16)
-
-        def columns(step, carry):
-            here = pl.ds(pl.multiple_of(step * tile, tile), tile)
-            high, low = split(held[at, here, :])
-            by_col[: 4 * CAP, here] = dot(col_pick, high, rows_dims).astype(BF16)
-            by_col[4 * CAP :, here] = dot(col_pick, low, rows_dims).astype(BF16)
-            return carry
-
-        lax.fori_loop(0, LOC // tile, columns, 0)
+        for side in range(2):
+            lanes = pl.ds(side * mid, mid)
+            full = (at != 4) & (at != (3, 5)[side])
+
+            @pl.when(full)
+            def _():
+                high, low = columns_of(0, at, lanes)
+                by_col[: 4 * CAP, lanes] = high.astype(BF16)
+                by_col[4 * CAP :, lanes] = low.astype(BF16)
+
+            @pl.when(jnp.logical_not(full))
+            def _():
+                high, low = split(strained[jnp.where(at == 4, 2 + side, 1 - side)])
+                by_col[: 4 * CAP, lanes] = high
+                by_col[4 * CAP :, lanes] = low
 
         def rows(step, carry):
             here = pl.ds(pl.multiple_of(step * tile, tile), tile)
@@ -476,32 +541,47 @@
         lax.fori_loop(0, LOC // tile, rows, 0)
         return carry
 
-    for side in range(2):
+    for turn in range(2):
         for way in range(2):
-            ring(0, side, way).start()
+            ring(0, way, (turn + way) % 2).start()
     for source in range(2):
         slots = lax.broadcasted_iota(jnp.int32, pick.shape[1:], 0)
         pick[source] = (slots == row_ref[source]).astype(F32).astype(BF16)
     front.wait()
 
     def event(number, carry):
-        @pl.when(number % 2 == 1)
-        def _():
-            step = (number + 1) // 2
-            for side in range(2):
-                arrived(8 - step, side)
-
-                @pl.when(step < 4 - side)
-                def _():
-                    ring(8 - step, side, 0).start()
-
-                @pl.when(step < 4)
-                def _():
-                    arrived(step, side)
-
-                    @pl.when(step < 3 + side)
-                    def _():
-                        ring(step, side, 1).start()
+        @pl.when(number == 1)
+        def _():
+            for turn in range(2):
+                for way in range(2):
+                    at, side = (7, 1)[way], (turn + way) % 2
+                    arrived(at, side)
+                    ring(at, way, side).start()
+
+        @pl.when(number == 3)
+        def _():
+            for way in range(2):
+                at, side = (6, 2)[way], way
+                arrived(at, side)
+                ring(at, way, side).start()
+            for way in range(2):
+                at, side = (6, 2)[way], 1 - way
+                arrived(at, side)
+                strain(at, side, way, way)
+
+        @pl.when(number == 5)
+        def _():
+            for way in range(2):
+                at, side = (5, 3)[way], way
+                arrived(at, side)
+                strain(at, side, way, 2 + way)
+            for way in range(2):
+                less(way, way).wait_recv()
+
+        @pl.when(number == 7)
+        def _():
+            for way in range(2):
+                less(2 + way, way).wait_recv()
 
         @pl.when(number >= 4)
         def _():
@@ -524,11 +604,13 @@
         return carry
 
     lax.fori_loop(4, 8, settle, 0)
-    for side in range(2):
-        for at in (0, 7, 6, 5)[: 4 - side]:
-            ring(at, side, 0).wait_send()
-        for at in (0, 1, 2, 3)[: 3 + side]:
-            ring(at, side, 1).wait_send()
+    for way in range(2):
+        for at in ((0, 7), (0, 1))[way]:
+            for side in range(2):
+                ring(at, way, side).wait_send()
+        ring((6, 2)[way], way, way).wait_send()
+        less(way, way).wait_send()
+        less(2 + way, way).wait_send()
 
 
 def exchange(block, parent, row_slots, col_slots, row_land, col_land):
@@ -539,7 +621,9 @@
         in_specs=[pl.BlockSpec(memory_space=pl.ANY)] * 2 + [pl.BlockSpec(memory_space=pltpu.VMEM)] * 4,
         out_specs=pl.BlockSpec(memory_space=pltpu.VMEM),
         scratch_shapes=[
-            pltpu.VMEM((8, rows, cols), F32),
+            pltpu.VMEM((7, rows, cols), F32),
+            pltpu.VMEM((4, 4 * CAP, SUB), F32),
+            pltpu.VMEM((4, 4 * CAP, SUB), F32),
             pltpu.VMEM((4, 4 * CAP, LOC), F32),
             pltpu.VMEM((8, 2, 4 * CAP, SUB), F32),
             pltpu.VMEM((2, LOC, rows), BF16),
@@ -551,6 +635,8 @@
             pltpu.SemaphoreType.DMA,
             pltpu.SemaphoreType.DMA((2, 8, 2)),
             pltpu.SemaphoreType.DMA((8, 2)),
+            pltpu.SemaphoreType.DMA((4,)),
+            pltpu.SemaphoreType.DMA((4,)),
             pltpu.SemaphoreType.DMA((8,)),
             pltpu.SemaphoreType.DMA((8,)),
             pltpu.SemaphoreType.DMA((8,)),
@@ -573,7 +659,8 @@
     slot = (((target // 8) * 4 + target % 4) * 2 + side) * CAP + rank
     row_slots = jnp.where(target // 4 % 2 == row // 4, slot, -1).reshape(2, 1, 2 * SUB)
     target, rank = send_slots(lax.dynamic_index_in_dim(mine.reshape(4, 4, SUB), col // 4, 0, keepdims=False))
-    col_slots = jnp.where(target % 4 == col % 4, (target // 4) * CAP + rank, -1).reshape(4, 1, SUB)
+    stops = (col + jnp.array([0, 1, 3], jnp.int32))[:, None, None] % 4
+    col_slots = jnp.where(target % 4 == stops, (target // 4) * CAP + rank, -1).reshape(3, 4, 1, SUB)
 
     row_land = landing(maps, group).reshape(2, 2, 1, SUB)
     col_land = landing(maps, col).reshape(2, 4, 4, CAP).transpose(0, 2, 1, 3).reshape(2, 4, 1, 4 * CAP)

time: 311 us -> 298 us (0.958)
  the two profiles are of different devices: /device:TPU:73 before, /device:TPU:225 now
where the time goes in v1:
time: 298 us; the launch traced here: 297 us
  Pallas kernels  279 us (94%)
  matrix products  7.78 us (3%)
  other arithmetic  5.38 us (2%)
  local copies, waits for them, and re-layouts  4.16 us (1%)
    pallas_call x1, Pallas kernels, exchange(): pl.pallas_call(exchange_kernel, out_shape=jax.ShapeDtypeStruct(parent.sha...  181 us
    pallas_call x1, Pallas kernels, spread(): pl.pallas_call(spread_kernel, out_shape=[jax.ShapeDtypeStruct(f.shape, F3...  97.5 us

profile of v1, /device:TPU:225, one launch (start us, length us, event | category | flops | bytes accessed | tf_op | source)
XLA Modules:
  0.0 297.3 jit_solution(3902275947443418158)
XLA Ops:
  0.7 0.7 and_select_fusion.5
  1.4 1.1 fusion.4
  2.5 1.1 fusion.5
  3.6 0.9 fusion.11
  4.5 1.2 select_reduce_fusion
  5.7 0.7 reshape.146.col_land_ref
  6.4 0.7 sub.67.row_land_ref
  7.1 0.9 copy.26
  8.1 0.2 fusion.2
  8.3 0.8 compare_select_fusion.3.row_ref
  9.1 0.2 fusion.3
  9.4 0.7 compare_select_fusion.col_ref
  10.1 181.4 %exchange.1 = f32[1024,1024]{1,0:T(8,128)} custom-call(f32[1024,512]{1,0:T(8,128)} %bitcast.53, f32[1024,1024]{1,0:T(8,128)} %parent_ref.1, s32[2,1,1024]{2,1,0:T(1,128)} %compare_select_fusion.3.row_ref, s32[3,4,1,512]{3,2,1,0:T(1,128)} %compare_select_fusion.col_ref, s32[2,2,1,512]{3,2,1,0:T(1,128)} %sub.67.row_land_ref, ...), custom_call_target="tpu_custom_call" | custom-call | tf_op jit(solution)/shard_map/exchange/pallas_call | solution.py:618
  191.5 0.0 copy-start
  191.5 1.8 slice.3.a_ref
  193.3 0.0 copy-done
  193.3 0.0 copy-start.1
  193.3 0.3 panel.1.f_ref
  193.7 97.5 %spread.1 = (f32[1024,512]{1,0:T(8,128)S(1)}, f32[1024,512]{1,0:T(8,128)S(1)}) custom-call(f32[1024,512]{1,0:T(8,128)S(1)} %panel.1.f_ref), custom_call_target="tpu_custom_call" | custom-call | tf_op jit(solution)/shard_map/spread/pallas_call | solution.py:351
  291.2 0.0 copy-done.1
  291.2 5.0 %convolution_subtract_fusion = f32[1024,1024]{1,0:T(8,128)} fusion(f32[1024,1024]{1,0:T(8,128)S(1)} %copy-done.1, f32[1024,512]{1,0:T(8,128)S(1)} %get-tuple-element.4, f32[1024,512]{1,0:T(8,128)S(1)} %get-tuple-element.5), kind=kOutput, calls=%fused_computation.4 | convolution fusion | flops 3222274048 | bytes 12582912 | tf_op jit(solution)/shard_map/dot_general | solution.py:671
  296.2 1.1 convert_element_type.14
  (14 shorter events, 0.2 us)
Async XLA Ops:
  191.5 1.8 copy-start
  193.3 97.9 %copy-start.1 = (f32[1024,1024]{1,0:T(8,128)S(1)}, f32[1024,1024]{1,0:T(8,128)}, u32[]{:S(2)}) copy-start(f32[1024,1024]{1,0:T(8,128)} %exchange.1) | copy-start | bytes 12582916

commit v2 on v1

--- a/solution.py
+++ b/solution.py
@@ -22,26 +22,6 @@
 
 def dot(left, right, dims):
     return lax.dot_general(left, right, (dims, ((), ())), preferred_element_type=F32)
-
-
-def before(flags):
-    size = flags.shape[-1]
-    upper = jnp.arange(size)[:, None] < jnp.arange(size)[None, :]
-    return jnp.dot(flags.astype(BF16), upper.astype(BF16), preferred_element_type=F32).astype(jnp.int32)
-
-
-def send_slots(parents):
-    targets = parents // LOC
-    member = targets[:, None, :] == jnp.arange(GROUPS, dtype=jnp.int32)[None, :, None]
-    rank = jnp.sum(before(member) * member.astype(jnp.int32), axis=1)
-    return targets, rank
-
-
-def landing(parents, mine):
-    member = parents // LOC == mine
-    rank = jnp.where(member, before(member), -1)
-    hit = rank[:, :, None, :] == jnp.arange(CAP, dtype=jnp.int32)[None, None, :, None]
-    return jnp.sum(jnp.where(hit, (parents % LOC + 1)[:, :, None, :], 0), axis=-1) - 1
 
 
 def place():
@@ -135,7 +115,7 @@
     return dot(left_high, right_high, dims) + (dot(left_high, right_low, dims) + dot(left_low, right_high, dims))
 
 
-def panel_kernel(a_ref, inv_ref, f_ref, d_ref, l_ref, send, recv, own):
+def panel_kernel(front_ref, inv_ref, f_ref, a_ref, d_ref, l_ref, send, recv, own, first):
     half, z_hi, x, y, z_lo = place()
     source, children, parent, _ = group_tree(half, z_hi, x, y, z_lo, 0, 0, 0)
     active = (y == 0) & (z_lo == 0)
@@ -143,10 +123,14 @@
 
     @pl.when(active)
     def _():
+        mine = pltpu.make_async_copy(front_ref.at[:, pl.ds(0, PANEL)], a_ref, first)
+        mine.start()
+
         @pl.when(jnp.logical_not(source))
         def _():
             pl.semaphore_signal(barrier, inc=1, device_id=parent, device_id_type=MESH)
 
+        mine.wait()
         wait_for(barrier, count(children))
 
         def piece(ref, block):
@@ -160,9 +144,9 @@
         for block in range(1, BLOCKS):
             @pl.when(source)
             def _():
-                mine = pltpu.make_async_copy(piece(a_ref, block), piece(d_ref, block), own)
-                mine.start()
-                mine.wait()
+                copied = pltpu.make_async_copy(piece(a_ref, block), piece(d_ref, block), own)
+                copied.start()
+                copied.wait()
 
             @pl.when(jnp.logical_not(source))
             def _():
@@ -197,26 +181,28 @@
                     copy(block, number).wait_send()
 
 
-def panel(a, inverse_blocks):
+def panel(front, inverse_blocks):
     return pl.pallas_call(
         panel_kernel,
-        out_shape=jax.ShapeDtypeStruct(a.shape, F32),
-        in_specs=[pl.BlockSpec(memory_space=pltpu.VMEM)] * 2,
+        out_shape=jax.ShapeDtypeStruct((LOC, PANEL), F32),
+        in_specs=[pl.BlockSpec(memory_space=pl.ANY), pl.BlockSpec(memory_space=pltpu.VMEM)],
         out_specs=pl.BlockSpec(memory_space=pltpu.VMEM),
         scratch_shapes=[
+            pltpu.VMEM((LOC, PANEL), F32),
             pltpu.VMEM((PANEL, PANEL), F32),
             pltpu.VMEM((PANEL, PANEL), F32),
             pltpu.SemaphoreType.DMA((4, BLOCKS - 1)),
             pltpu.SemaphoreType.DMA((BLOCKS - 1,)),
             pltpu.SemaphoreType.DMA,
+            pltpu.SemaphoreType.DMA,
         ],
         compiler_params=pltpu.CompilerParams(collective_id=0, has_side_effects=True, vmem_limit_bytes=24 * 2**20),
         name="panel",
-    )(a, inverse_blocks)
-
-
-CHUNK = 32
-STEP = 2
+    )(front, inverse_blocks)
+
+
+CHUNK = 16
+STEP = 3
 
 
 def spread_kernel(f_ref, row_ref, col_ref, recv_z, recv_y, recv_g, send_z, send_y, send_g, own):
@@ -368,8 +354,8 @@
 
 
 def exchange_kernel(
-    x_ref, parent_ref, row_ref, col_ref, row_land_ref, col_land_ref, out_ref,
-    held, strained, passed, packed, landed, pick, by_col, parts, by_row, put,
+    x_ref, parent_ref, maps_ref, out_ref,
+    col_ref, row_land_ref, col_land_ref, upper, held, strained, passed, packed, landed, pick, by_col, parts, by_row, put,
     own, first, ring_sent, ring_got, less_sent, less_got, sent, got, kept,
 ):
     half, z_hi, x, y, z_lo = place()
@@ -544,9 +530,67 @@
     for turn in range(2):
         for way in range(2):
             ring(0, way, (turn + way) % 2).start()
+    upper[...] = (
+        lax.broadcasted_iota(jnp.int32, (SUB, SUB), 0) < lax.broadcasted_iota(jnp.int32, (SUB, SUB), 1)
+    ).astype(F32).astype(BF16)
+
+    def before(member):
+        return dot(member.astype(F32).astype(BF16), upper[...], ((1,), (0,)))
+
+    def send_slots(parents):
+        targets = parents >> 10
+        member = targets == lax.broadcasted_iota(jnp.int32, (GROUPS, SUB), 0)
+        rank = jnp.sum(jnp.where(member, before(member), 0.0), axis=0, keepdims=True)
+        return targets, rank.astype(jnp.int32)
+
     for source in range(2):
-        slots = lax.broadcasted_iota(jnp.int32, pick.shape[1:], 0)
-        pick[source] = (slots == row_ref[source]).astype(F32).astype(BF16)
+        for sub in range(2):
+            targets, rank = send_slots(maps_ref[half, pl.ds(source * 8 + x * 2 + sub, 1), :])
+            slot = (((targets >> 3) * 4 + (targets & 3)) * 2 + sub) * CAP + rank
+            slot = jnp.where(((targets >> 2) & 1) == z_hi, slot, -1)
+            slots = lax.broadcasted_iota(jnp.int32, (LOC, SUB), 0)
+            pick[source, :, sub * SUB : (sub + 1) * SUB] = (slots == slot).astype(F32).astype(BF16)
+    for source in range(4):
+        targets, rank = send_slots(maps_ref[half, pl.ds(y * 4 + source, 1), :])
+        for which, stop in enumerate((0, 1, 3)):
+            slot = (targets >> 2) * CAP + rank
+            col_ref[which, source] = jnp.where((targets & 3) == (z_lo + stop) % 4, slot, -1)
+
+    def landing(child, mine, store):
+        parents = maps_ref[child]
+        member = (parents >> 10) == mine
+        rank = jnp.where(member, before(member).astype(jnp.int32), -1)
+        place = (parents & (LOC - 1)) + 1
+        slots = lax.broadcasted_iota(jnp.int32, (2 * CAP, SUB), 0)
+        line = lax.broadcasted_iota(jnp.int32, (8, SUB), 0)
+
+        def side(block, shift):
+            values = place[block : block + 1]
+            values = jnp.where(line == 0, values >> 5, jnp.where(line == 1, values & 31, 0)).astype(F32).astype(BF16)
+            mine_rank = rank[block : block + 1]
+            hit = slots == jnp.where(mine_rank < 0, -1, mine_rank + shift)
+            return dot(values, hit.astype(F32).astype(BF16), rows_dims)
+
+        store(lambda first, second: (lambda both: (both[0:1] * 32.0 + both[1:2]).astype(jnp.int32) - 1)(
+            side(first, 0) + side(second, CAP)
+        ))
+
+    for child in range(2):
+        def rows_land(pair):
+            for source in range(2):
+                for at_x in range(4):
+                    block = source * 8 + at_x * 2
+                    row_land_ref[child, source, :, at_x * 128 : (at_x + 1) * 128] = pair(block, block + 1)
+
+        def cols_land(pair):
+            for source in range(4):
+                for at_y in range(2):
+                    col_land_ref[child, source, :, at_y * 128 : (at_y + 1) * 128] = pair(
+                        at_y * 8 + source, at_y * 8 + 4 + source
+                    )
+
+        landing(child, half * 8 + z_hi * 4 + x, rows_land)
+        landing(child, y * 4 + z_lo, cols_land)
     front.wait()
 
     def event(number, carry):
@@ -613,14 +657,18 @@
         less(2 + way, way).wait_send()
 
 
-def exchange(block, parent, row_slots, col_slots, row_land, col_land):
+def exchange(block, parent, maps):
     rows, cols = block.shape
     return pl.pallas_call(
         exchange_kernel,
         out_shape=jax.ShapeDtypeStruct(parent.shape, F32),
-        in_specs=[pl.BlockSpec(memory_space=pl.ANY)] * 2 + [pl.BlockSpec(memory_space=pltpu.VMEM)] * 4,
+        in_specs=[pl.BlockSpec(memory_space=pl.ANY)] * 2 + [pl.BlockSpec(memory_space=pltpu.VMEM)],
         out_specs=pl.BlockSpec(memory_space=pltpu.VMEM),
         scratch_shapes=[
+            pltpu.VMEM((3, 4, 1, SUB), jnp.int32),
+            pltpu.VMEM((2, 2, 1, SUB), jnp.int32),
+            pltpu.VMEM((2, 4, 1, 4 * CAP), jnp.int32),
+            pltpu.VMEM((SUB, SUB), BF16),
             pltpu.VMEM((7, rows, cols), F32),
             pltpu.VMEM((4, 4 * CAP, SUB), F32),
             pltpu.VMEM((4, 4 * CAP, SUB), F32),
@@ -643,30 +691,12 @@
         ],
         compiler_params=pltpu.CompilerParams(collective_id=2, has_side_effects=True, vmem_limit_bytes=63 * 2**20),
         name="exchange",
-    )(block, parent, row_slots, col_slots, row_land, col_land)
+    )(block, parent, maps)
 
 
 def local(parent_front, child_blocks, row_maps, inverse_blocks):
-    half, row, col = lax.axis_index("half"), lax.axis_index("row"), lax.axis_index("col")
-    group = half * 8 + row
-    maps = row_maps.reshape(2, -1, SUB)
-
-    mine = lax.dynamic_index_in_dim(maps, half, 0, keepdims=False)
-    shards = mine.reshape(2, 4, 2 * SUB)
-    target, rank = send_slots(lax.dynamic_index_in_dim(shards, row % 4, 1, keepdims=False).reshape(4, SUB))
-    target, rank = target.reshape(2, 2, SUB), rank.reshape(2, 2, SUB)
-    side = jnp.arange(2, dtype=jnp.int32)[:, None]
-    slot = (((target // 8) * 4 + target % 4) * 2 + side) * CAP + rank
-    row_slots = jnp.where(target // 4 % 2 == row // 4, slot, -1).reshape(2, 1, 2 * SUB)
-    target, rank = send_slots(lax.dynamic_index_in_dim(mine.reshape(4, 4, SUB), col // 4, 0, keepdims=False))
-    stops = (col + jnp.array([0, 1, 3], jnp.int32))[:, None, None] % 4
-    col_slots = jnp.where(target % 4 == stops, (target // 4) * CAP + rank, -1).reshape(3, 4, 1, SUB)
-
-    row_land = landing(maps, group).reshape(2, 2, 1, SUB)
-    col_land = landing(maps, col).reshape(2, 4, 4, CAP).transpose(0, 2, 1, 3).reshape(2, 4, 1, 4 * CAP)
-    assembled = exchange(child_blocks[0], parent_front, row_slots, col_slots, row_land, col_land)
-
-    factor = panel(assembled[:, :PANEL], inverse_blocks)
+    assembled = exchange(child_blocks[0], parent_front, row_maps.reshape(2, -1, SUB))
+    factor = panel(assembled, inverse_blocks)
     factor_rows, factor_cols = spread(factor)
     product = lax.dot_general(
         factor_rows, factor_cols, (((1,), (1,)), ((), ())), precision=lax.Precision.HIGH, preferred_element_type=F32

time: 298 us -> 291 us (0.977)
  other arithmetic: 5.38 us -> 1.1 us
where the time goes in v2:
time: 291 us; the launch traced here: 290 us
  Pallas kernels  279 us (96%)
  matrix products  5.04 us (2%)
  local copies, waits for them, and re-layouts  3.67 us (1%)
    pallas_call x1, Pallas kernels, exchange(): pl.pallas_call(exchange_kernel, out_shape=jax.ShapeDtypeStruct(parent.sha...  181 us
    pallas_call x1, Pallas kernels, spread(): pl.pallas_call(spread_kernel, out_shape=[jax.ShapeDtypeStruct(f.shape, F3...  97.9 us

profile of v2, /device:TPU:225, one launch (start us, length us, event | category | flops | bytes accessed | tf_op | source)
XLA Modules:
  0.0 289.8 jit_solution(9035877075199724318)
XLA Ops:
  0.6 1.5 copy.8
  2.1 0.0 copy-start.2
  2.1 181.2 %exchange.1.front_ref = f32[1024,1024]{1,0:T(8,128)} custom-call(f32[1024,512]{1,0:T(8,128)} %bitcast.7, f32[1024,1024]{1,0:T(8,128)} %parent_ref.1, s32[2,16,512]{2,1,0:T(8,128)} %bitcast.8), custom_call_target="tpu_custom_call" | custom-call | tf_op jit(solution)/shard_map/exchange/pallas_call | solution.py:662
  183.3 0.0 copy-done.2
  183.4 0.0 copy-start
  183.4 2.2 copy-done
  185.5 0.0 copy-start.1
  185.5 0.2 panel.1.f_ref
  185.7 97.9 %spread.1 = (f32[1024,512]{1,0:T(8,128)S(1)}, f32[1024,512]{1,0:T(8,128)S(1)}) custom-call(f32[1024,512]{1,0:T(8,128)S(1)} %panel.1.f_ref), custom_call_target="tpu_custom_call" | custom-call | tf_op jit(solution)/shard_map/spread/pallas_call | solution.py:337
  283.6 0.0 copy-done.1
  283.6 5.0 %convolution_subtract_fusion = f32[1024,1024]{1,0:T(8,128)} fusion(f32[1024,1024]{1,0:T(8,128)S(1)} %copy-done.1, f32[1024,512]{1,0:T(8,128)S(1)} %get-tuple-element.4, f32[1024,512]{1,0:T(8,128)S(1)} %get-tuple-element.5), kind=kOutput, calls=%fused_computation | convolution fusion | flops 3222274048 | bytes 12582912 | tf_op jit(solution)/shard_map/dot_general | solution.py:701
  288.7 1.1 convert_element_type.3
Async XLA Ops:
  2.1 181.2 %copy-start.2 = (f32[4,128,128]{2,1,0:T(8,128)S(1)}, f32[4,128,128]{2,1,0:T(8,128)}, u32[]{:S(2)}) copy-start(f32[4,128,128]{2,1,0:T(8,128)} %inv_ref.1) | copy-start | bytes 786436
  183.4 2.2 copy-start
  185.5 98.1 %copy-start.1 = (f32[1024,1024]{1,0:T(8,128)S(1)}, f32[1024,1024]{1,0:T(8,128)}, u32[]{:S(2)}) copy-start(f32[1024,1024]{1,0:T(8,128)} %exchange.1.front_ref) | copy-start | bytes 12582916

commit v3 on v2

--- a/solution.py
+++ b/solution.py
@@ -115,7 +115,7 @@
     return dot(left_high, right_high, dims) + (dot(left_high, right_low, dims) + dot(left_low, right_high, dims))
 
 
-def panel_kernel(front_ref, inv_ref, f_ref, a_ref, d_ref, l_ref, send, recv, own, first):
+def panel_kernel(a_ref, inv_ref, f_ref, d_ref, l_ref, send, recv, own):
     half, z_hi, x, y, z_lo = place()
     source, children, parent, _ = group_tree(half, z_hi, x, y, z_lo, 0, 0, 0)
     active = (y == 0) & (z_lo == 0)
@@ -123,14 +123,10 @@
 
     @pl.when(active)
     def _():
-        mine = pltpu.make_async_copy(front_ref.at[:, pl.ds(0, PANEL)], a_ref, first)
-        mine.start()
-
         @pl.when(jnp.logical_not(source))
         def _():
             pl.semaphore_signal(barrier, inc=1, device_id=parent, device_id_type=MESH)
 
-        mine.wait()
         wait_for(barrier, count(children))
 
         def piece(ref, block):
@@ -181,28 +177,26 @@
                     copy(block, number).wait_send()
 
 
-def panel(front, inverse_blocks):
+def panel(a, inverse_blocks):
     return pl.pallas_call(
         panel_kernel,
-        out_shape=jax.ShapeDtypeStruct((LOC, PANEL), F32),
-        in_specs=[pl.BlockSpec(memory_space=pl.ANY), pl.BlockSpec(memory_space=pltpu.VMEM)],
+        out_shape=jax.ShapeDtypeStruct(a.shape, F32),
+        in_specs=[pl.BlockSpec(memory_space=pltpu.VMEM)] * 2,
         out_specs=pl.BlockSpec(memory_space=pltpu.VMEM),
         scratch_shapes=[
-            pltpu.VMEM((LOC, PANEL), F32),
             pltpu.VMEM((PANEL, PANEL), F32),
             pltpu.VMEM((PANEL, PANEL), F32),
             pltpu.SemaphoreType.DMA((4, BLOCKS - 1)),
             pltpu.SemaphoreType.DMA((BLOCKS - 1,)),
             pltpu.SemaphoreType.DMA,
-            pltpu.SemaphoreType.DMA,
         ],
         compiler_params=pltpu.CompilerParams(collective_id=0, has_side_effects=True, vmem_limit_bytes=24 * 2**20),
         name="panel",
-    )(front, inverse_blocks)
-
-
-CHUNK = 16
-STEP = 3
+    )(a, inverse_blocks)
+
+
+CHUNK = 32
+STEP = 2
 
 
 def spread_kernel(f_ref, row_ref, col_ref, recv_z, recv_y, recv_g, send_z, send_y, send_g, own):
@@ -354,7 +348,7 @@
 
 
 def exchange_kernel(
-    x_ref, parent_ref, maps_ref, out_ref,
+    x_ref, parent_ref, maps_ref, out_ref, panel_ref,
     col_ref, row_land_ref, col_land_ref, upper, held, strained, passed, packed, landed, pick, by_col, parts, by_row, put,
     own, first, ring_sent, ring_got, less_sent, less_got, sent, got, kept,
 ):
@@ -522,6 +516,7 @@
                 both = by_row[at_of(number) % 4, child, here, :] + rows_of(number, child, step)
                 total = total + dot(both, put[child], rows_dims)
             out_ref[here, :] = total
+            panel_ref[here, :] = total[:, :PANEL]
             return carry
 
         lax.fori_loop(0, LOC // tile, rows, 0)
@@ -537,6 +532,9 @@
     def before(member):
         return dot(member.astype(F32).astype(BF16), upper[...], ((1,), (0,)))
 
+    def entries(block):
+        return maps_ref[pl.ds(half, 1), pl.ds(pl.multiple_of(block * SUB, SUB), SUB)]
+
     def send_slots(parents):
         targets = parents >> 10
         member = targets == lax.broadcasted_iota(jnp.int32, (GROUPS, SUB), 0)
@@ -545,19 +543,21 @@
 
     for source in range(2):
         for sub in range(2):
-            targets, rank = send_slots(maps_ref[half, pl.ds(source * 8 + x * 2 + sub, 1), :])
+            targets, rank = send_slots(entries(source * 8 + x * 2 + sub))
             slot = (((targets >> 3) * 4 + (targets & 3)) * 2 + sub) * CAP + rank
             slot = jnp.where(((targets >> 2) & 1) == z_hi, slot, -1)
             slots = lax.broadcasted_iota(jnp.int32, (LOC, SUB), 0)
             pick[source, :, sub * SUB : (sub + 1) * SUB] = (slots == slot).astype(F32).astype(BF16)
     for source in range(4):
-        targets, rank = send_slots(maps_ref[half, pl.ds(y * 4 + source, 1), :])
+        targets, rank = send_slots(entries(y * 4 + source))
         for which, stop in enumerate((0, 1, 3)):
             slot = (targets >> 2) * CAP + rank
             col_ref[which, source] = jnp.where((targets & 3) == (z_lo + stop) % 4, slot, -1)
 
     def landing(child, mine, store):
-        parents = maps_ref[child]
+        parents = jnp.concatenate(
+            [maps_ref[child : child + 1, block * SUB : (block + 1) * SUB] for block in range(GROUPS)], axis=0
+        )
         member = (parents >> 10) == mine
         rank = jnp.where(member, before(member).astype(jnp.int32), -1)
         place = (parents & (LOC - 1)) + 1
@@ -661,9 +661,9 @@
     rows, cols = block.shape
     return pl.pallas_call(
         exchange_kernel,
-        out_shape=jax.ShapeDtypeStruct(parent.shape, F32),
+        out_shape=[jax.ShapeDtypeStruct(parent.shape, F32), jax.ShapeDtypeStruct((LOC, PANEL), F32)],
         in_specs=[pl.BlockSpec(memory_space=pl.ANY)] * 2 + [pl.BlockSpec(memory_space=pltpu.VMEM)],
-        out_specs=pl.BlockSpec(memory_space=pltpu.VMEM),
+        out_specs=[pl.BlockSpec(memory_space=pltpu.VMEM)] * 2,
         scratch_shapes=[
             pltpu.VMEM((3, 4, 1, SUB), jnp.int32),
             pltpu.VMEM((2, 2, 1, SUB), jnp.int32),
@@ -695,8 +695,8 @@
 
 
 def local(parent_front, child_blocks, row_maps, inverse_blocks):
-    assembled = exchange(child_blocks[0], parent_front, row_maps.reshape(2, -1, SUB))
-    factor = panel(assembled, inverse_blocks)
+    assembled, columns = exchange(child_blocks[0], parent_front, row_maps)
+    factor = panel(columns, inverse_blocks)
     factor_rows, factor_cols = spread(factor)
     product = lax.dot_general(
         factor_rows, factor_cols, (((1,), (1,)), ((), ())), precision=lax.Precision.HIGH, preferred_element_type=F32

time: 291 us -> 289 us (level)
  no operation moved by 1% of the time
where the time goes in v3:
time: 289 us; the launch traced here: 288 us
  Pallas kernels  280 us (97%)
  matrix products  5.03 us (2%)
    pallas_call x1, Pallas kernels, exchange(): pl.pallas_call(exchange_kernel, out_shape=[jax.ShapeDtypeStruct(parent.sh...  182 us
    pallas_call x1, Pallas kernels, spread(): pl.pallas_call(spread_kernel, out_shape=[jax.ShapeDtypeStruct(f.shape, F3...  97.8 us

profile of v3, /device:TPU:225, one launch (start us, length us, event | category | flops | bytes accessed | tf_op | source)
XLA Modules:
  0.0 288.4 jit_solution(9240329384384136207)
XLA Ops:
  0.6 0.0 copy-start.1
  0.6 182.0 %exchange.1 = (f32[1024,1024]{1,0:T(8,128)}, f32[1024,512]{1,0:T(8,128)}) custom-call(f32[1024,512]{1,0:T(8,128)} %bitcast.3, f32[1024,1024]{1,0:T(8,128)} %parent_ref.1, s32[2,8192]{1,0:T(2,128)} %maps_ref.1), custom_call_target="tpu_custom_call" | custom-call | tf_op jit(solution)/shard_map/exchange/pallas_call | solution.py:662
  182.7 0.0 copy-done.1
  182.7 0.0 copy-start
  182.7 1.6 copy-done
  184.3 0.0 copy-start.2
  184.3 0.1 panel.1.f_ref
  184.4 97.8 %spread.1 = (f32[1024,512]{1,0:T(8,128)S(1)}, f32[1024,512]{1,0:T(8,128)S(1)}) custom-call(f32[1024,512]{1,0:T(8,128)S(1)} %panel.1.f_ref), custom_call_target="tpu_custom_call" | custom-call | tf_op jit(solution)/shard_map/spread/pallas_call | solution.py:331
  282.3 0.0 copy-done.2
  282.3 5.0 %convolution_subtract_fusion = f32[1024,1024]{1,0:T(8,128)} fusion(f32[1024,1024]{1,0:T(8,128)S(1)} %copy-done.2, f32[1024,512]{1,0:T(8,128)S(1)} %get-tuple-element.8, f32[1024,512]{1,0:T(8,128)S(1)} %get-tuple-element.9), kind=kOutput, calls=%fused_computation | convolution fusion | flops 3222274048 | bytes 12582912 | tf_op jit(solution)/shard_map/dot_general | solution.py:701
  287.3 1.1 convert_element_type.3
Async XLA Ops:
  0.6 182.0 %copy-start.1 = (f32[4,128,128]{2,1,0:T(8,128)S(1)}, f32[4,128,128]{2,1,0:T(8,128)}, u32[]{:S(2)}) copy-start(f32[4,128,128]{2,1,0:T(8,128)} %inv_ref.1) | copy-start | bytes 786436
  182.7 1.6 copy-start
  184.3 98.0 %copy-start.2 = (f32[1024,1024]{1,0:T(8,128)S(1)}, f32[1024,1024]{1,0:T(8,128)}, u32[]{:S(2)}) copy-start(f32[1024,1024]{1,0:T(8,128)} %get-tuple-element.6) | copy-start | bytes 12582916

commit v4 on v3

--- a/solution.py
+++ b/solution.py
@@ -132,37 +132,45 @@
         def piece(ref, block):
             return ref.at[pl.ds(block * WIDTH, WIDTH), pl.ds(0, block * WIDTH)]
 
-        def copy(block, number):
+        def copy(block, number, src=d_ref):
             return remote(
-                piece(d_ref, block), piece(d_ref, block), send.at[number, block - 1], recv.at[block - 1], children[number][1]
+                piece(src, block), piece(d_ref, block), send.at[number, block - 1], recv.at[block - 1], children[number][1]
             )
 
-        for block in range(1, BLOCKS):
-            @pl.when(source)
-            def _():
-                copied = pltpu.make_async_copy(piece(a_ref, block), piece(d_ref, block), own)
-                copied.start()
-                copied.wait()
-
-            @pl.when(jnp.logical_not(source))
-            def _():
+        def mine(block):
+            return pltpu.make_async_copy(piece(a_ref, block), piece(d_ref, block), own.at[block - 1])
+
+        @pl.when(source)
+        def _():
+            for block in range(1, BLOCKS):
+                for number in range(len(children)):
+                    copy(block, number, a_ref).start()
+                mine(block).start()
+
+        lower = lax.broadcasted_iota(jnp.int32, (WIDTH, WIDTH), 0) >= lax.broadcasted_iota(jnp.int32, (WIDTH, WIDTH), 1)
+        f_ref[:, :WIDTH] = outer(a_ref[:, :WIDTH], jnp.where(lower, inv_ref[0], 0.0))
+
+        @pl.when(source)
+        def _():
+            for block in range(1, BLOCKS):
+                mine(block).wait()
+
+        @pl.when(jnp.logical_not(source))
+        def _():
+            for block in range(1, BLOCKS):
                 copy(block, 0).wait_recv()
-
-            for number, (cond, _) in enumerate(children):
-                @pl.when(cond)
-                def _():
-                    copy(block, number).start()
-
-        lower = lax.broadcasted_iota(jnp.int32, (WIDTH, WIDTH), 0) >= lax.broadcasted_iota(jnp.int32, (WIDTH, WIDTH), 1)
+                for number, (cond, _) in enumerate(children):
+                    @pl.when(cond)
+                    def _():
+                        copy(block, number).start()
+
         for block in range(BLOCKS):
             inverse = jnp.where(lower, inv_ref[block], 0.0)
             here = pl.ds(block * WIDTH, WIDTH)
             done = pl.ds(0, block * WIDTH)
-            current = a_ref[:, here]
             if block > 0:
                 above = l_ref[here, done]
-                current = current - outer(f_ref[:, done], above)
-            f_ref[:, here] = outer(current, inverse)
+                f_ref[:, here] = outer(a_ref[:, here] - outer(f_ref[:, done], above), inverse)
             if block + 1 < BLOCKS:
                 below = pl.ds((block + 1) * WIDTH, PANEL - (block + 1) * WIDTH)
                 current = d_ref[below, here]
@@ -188,7 +196,7 @@
             pltpu.VMEM((PANEL, PANEL), F32),
             pltpu.SemaphoreType.DMA((4, BLOCKS - 1)),
             pltpu.SemaphoreType.DMA((BLOCKS - 1,)),
-            pltpu.SemaphoreType.DMA,
+            pltpu.SemaphoreType.DMA((BLOCKS - 1,)),
         ],
         compiler_params=pltpu.CompilerParams(collective_id=0, has_side_effects=True, vmem_limit_bytes=24 * 2**20),
         name="panel",

time: 289 us -> 289 us (level)
  no operation moved by 1% of the time
where the time goes in v4:
time: 289 us; the launch traced here: 288 us
  Pallas kernels  280 us (97%)
  matrix products  5.03 us (2%)
    pallas_call x1, Pallas kernels, exchange(): pl.pallas_call(exchange_kernel, out_shape=[jax.ShapeDtypeStruct(parent.sh...  182 us
    pallas_call x1, Pallas kernels, spread(): pl.pallas_call(spread_kernel, out_shape=[jax.ShapeDtypeStruct(f.shape, F3...  97.8 us

profile of v4, /device:TPU:225, one launch (start us, length us, event | category | flops | bytes accessed | tf_op | source)
XLA Modules:
  0.0 288.4 jit_solution(8207811365790478115)
XLA Ops:
  0.6 0.0 copy-start.1
  0.6 182.0 %exchange.1 = (f32[1024,1024]{1,0:T(8,128)}, f32[1024,512]{1,0:T(8,128)}) custom-call(f32[1024,512]{1,0:T(8,128)} %bitcast.3, f32[1024,1024]{1,0:T(8,128)} %parent_ref.1, s32[2,8192]{1,0:T(2,128)} %maps_ref.1), custom_call_target="tpu_custom_call" | custom-call | tf_op jit(solution)/shard_map/exchange/pallas_call | solution.py:670
  182.7 0.0 copy-done.1
  182.7 0.0 copy-start
  182.7 1.6 copy-done
  184.3 0.0 copy-start.2
  184.3 0.2 panel.1.f_ref
  184.4 97.8 %spread.1 = (f32[1024,512]{1,0:T(8,128)S(1)}, f32[1024,512]{1,0:T(8,128)S(1)}) custom-call(f32[1024,512]{1,0:T(8,128)S(1)} %panel.1.f_ref), custom_call_target="tpu_custom_call" | custom-call | tf_op jit(solution)/shard_map/spread/pallas_call | solution.py:339
  282.3 0.0 copy-done.2
  282.3 5.0 %convolution_subtract_fusion = f32[1024,1024]{1,0:T(8,128)} fusion(f32[1024,1024]{1,0:T(8,128)S(1)} %copy-done.2, f32[1024,512]{1,0:T(8,128)S(1)} %get-tuple-element.8, f32[1024,512]{1,0:T(8,128)S(1)} %get-tuple-element.9), kind=kOutput, calls=%fused_computation | convolution fusion | flops 3222274048 | bytes 12582912 | tf_op jit(solution)/shard_map/dot_general | solution.py:709
  287.3 1.1 convert_element_type.3
Async XLA Ops:
  0.6 182.0 %copy-start.1 = (f32[4,128,128]{2,1,0:T(8,128)S(1)}, f32[4,128,128]{2,1,0:T(8,128)}, u32[]{:S(2)}) copy-start(f32[4,128,128]{2,1,0:T(8,128)} %inv_ref.1) | copy-start | bytes 786436
  182.7 1.6 copy-start
  184.3 98.0 %copy-start.2 = (f32[1024,1024]{1,0:T(8,128)S(1)}, f32[1024,1024]{1,0:T(8,128)}, u32[]{:S(2)}) copy-start(f32[1024,1024]{1,0:T(8,128)} %get-tuple-element.6) | copy-start | bytes 12582916

commit v5 on v4

--- a/solution.py
+++ b/solution.py
@@ -641,11 +641,12 @@
 
         pack(number)
 
+        deliver(number)
+
         @pl.when((number >= 3) & (number < 7))
         def _():
             unpack_first(number - 3)
 
-        deliver(number)
         return carry
 
     lax.fori_loop(0, 8, event, 0)

time: 289 us -> 286 us (0.990)
  no operation moved by 1% of the time
where the time goes in v5:
time: 286 us
  Pallas kernels  278 us (97%)
  matrix products  5.03 us (2%)
    pallas_call x1, Pallas kernels, exchange(): pl.pallas_call(exchange_kernel, out_shape=[jax.ShapeDtypeStruct(parent.sh...  180 us
    pallas_call x1, Pallas kernels, spread(): pl.pallas_call(spread_kernel, out_shape=[jax.ShapeDtypeStruct(f.shape, F3...  97.8 us

profile of v5, /device:TPU:225, one launch (start us, length us, event | category | flops | bytes accessed | tf_op | source)
XLA Modules:
  0.0 286.3 jit_solution(6093786796302340465)
XLA Ops:
  0.6 0.0 copy-start.1
  0.6 179.9 %exchange.1 = (f32[1024,1024]{1,0:T(8,128)}, f32[1024,512]{1,0:T(8,128)}) custom-call(f32[1024,512]{1,0:T(8,128)} %bitcast.3, f32[1024,1024]{1,0:T(8,128)} %parent_ref.1, s32[2,8192]{1,0:T(2,128)} %maps_ref.1), custom_call_target="tpu_custom_call" | custom-call | tf_op jit(solution)/shard_map/exchange/pallas_call | solution.py:671
  180.6 0.0 copy-done.1
  180.6 0.0 copy-start
  180.6 1.6 copy-done
  182.2 0.0 copy-start.2
  182.2 0.2 panel.1.f_ref
  182.3 97.8 %spread.1 = (f32[1024,512]{1,0:T(8,128)S(1)}, f32[1024,512]{1,0:T(8,128)S(1)}) custom-call(f32[1024,512]{1,0:T(8,128)S(1)} %panel.1.f_ref), custom_call_target="tpu_custom_call" | custom-call | tf_op jit(solution)/shard_map/spread/pallas_call | solution.py:339
  280.2 0.0 copy-done.2
  280.2 5.0 %convolution_subtract_fusion = f32[1024,1024]{1,0:T(8,128)} fusion(f32[1024,1024]{1,0:T(8,128)S(1)} %copy-done.2, f32[1024,512]{1,0:T(8,128)S(1)} %get-tuple-element.8, f32[1024,512]{1,0:T(8,128)S(1)} %get-tuple-element.9), kind=kOutput, calls=%fused_computation | convolution fusion | flops 3222274048 | bytes 12582912 | tf_op jit(solution)/shard_map/dot_general | solution.py:710
  285.2 1.1 convert_element_type.3
Async XLA Ops:
  0.6 179.9 %copy-start.1 = (f32[4,128,128]{2,1,0:T(8,128)S(1)}, f32[4,128,128]{2,1,0:T(8,128)}, u32[]{:S(2)}) copy-start(f32[4,128,128]{2,1,0:T(8,128)} %inv_ref.1) | copy-start | bytes 786436
  180.6 1.6 copy-start
  182.2 98.0 %copy-start.2 = (f32[1024,1024]{1,0:T(8,128)S(1)}, f32[1024,1024]{1,0:T(8,128)}, u32[]{:S(2)}) copy-start(f32[1024,1024]{1,0:T(8,128)} %get-tuple-element.6) | copy-start | bytes 12582916
